TPU v7x, 32 devices: a whole 2x2x4 slice. The times are simulated.
32 devices in a mesh: dp: 8 (over z, y), tensor: 4 (over x, core).
Axes of the slice: x: 2, y: 2, z: 4, core: 2. Of those that a mesh axis runs over, the one named last changes fastest.
Arguments:
- layer_input: bfloat16 [16, 1024, 768], P('dp', 'tensor'), may hold values from -6 to 6
- cotangent: bfloat16 [16, 1024, 768], P('dp', 'tensor'), may hold values from -6 to 6
- segment_ids: int32 [16, 1024], P('dp'), may hold values from 0 to 15, never falling along the last dimension, each value on 1 to 512 neighbouring positions
- query_weight: bfloat16 [768, 768], P('dp', 'tensor'), may hold values from -0.21875 to 0.21875
- key_weight: bfloat16 [768, 768], P('dp', 'tensor'), may hold values from -0.21875 to 0.21875
- value_weight: bfloat16 [768, 768], P('dp', 'tensor'), may hold values from -0.21875 to 0.21875
- output_weight: bfloat16 [768, 768], P('tensor', 'dp'), may hold values from -0.875 to 0.875
- gate_weight: bfloat16 [768, 3072], P('dp', 'tensor'), may hold values from -0.21875 to 0.21875
- up_weight: bfloat16 [768, 3072], P('dp', 'tensor'), may hold values from -0.21875 to 0.21875
- down_weight: bfloat16 [3072, 768], P('tensor', 'dp'), may hold values from -0.109375 to 0.109375
- first_gain: float32 [768], replicated, may hold values from 0.5 to 1.5
- first_bias: float32 [768], replicated, may hold values from -1 to 1
- second_gain: float32 [768], replicated, may hold values from 0.5 to 1.5
- second_bias: float32 [768], replicated, may hold values from -1 to 1
Outputs:
- output: bfloat16 [16, 1024, 768], P('dp', 'tensor')
- grad_input: bfloat16 [16, 1024, 768], P('dp', 'tensor')
- grad_query_weight: float32 [768, 768], P('dp', 'tensor')
- grad_key_weight: float32 [768, 768], P('dp', 'tensor')
- grad_value_weight: float32 [768, 768], P('dp', 'tensor')
- grad_output_weight: float32 [768, 768], P('tensor', 'dp')
- grad_gate_weight: float32 [768, 3072], P('dp', 'tensor')
- grad_up_weight: float32 [768, 3072], P('dp', 'tensor')
- grad_down_weight: float32 [3072, 768], P('tensor', 'dp')
- grad_first_gain: float32 [768], replicated
- grad_first_bias: float32 [768], replicated
- grad_second_gain: float32 [768], replicated
- grad_second_bias: float32 [768], replicated
Inputs may be any that keep to these rules, and one draw needn't show every extreme that they name: `segment_ids`: ids never fall along a packed row and attention only joins tokens of equal id within one row; a document has 1 to 512 tokens, and some document has exactly that many.
All inputs are finite; a program needn't handle non-finite values.
Results may differ from a plain program's by a relative error of at most 0.023.
Values may be sent and summed in bfloat16 or wider, within the bound.
A program may use at most 128 MiB of HBM per device.

v0:
```python
import jax
import jax.numpy as jnp
from jax import lax
from jax.sharding import PartitionSpec as P

HD = 64
eps_norm = 1e-06
rope_base = 1000.0
mask_fill = -1e30


def layer_norm(field_rows, gain_vec, bias_vec):
    row_mean = jnp.mean(field_rows, axis=-1, keepdims=True)
    centred = field_rows - row_mean
    variance = jnp.mean(centred * centred, axis=-1, keepdims=True)
    return centred * lax.rsqrt(variance + eps_norm) * gain_vec + bias_vec


def rotary_tables(length, head_dim):
    half_dim = head_dim // 2
    frequency = rope_base ** (-(2.0 * jnp.arange(half_dim, dtype=jnp.float32)) / head_dim)
    angles = jnp.arange(length, dtype=jnp.float32)[:, None] * frequency[None, :]
    return (jnp.cos(angles), jnp.sin(angles))


def rotate(heads_data, cos_table, sine_table):
    half_dim = heads_data.shape[-1] // 2
    first_half = heads_data[..., :half_dim]
    second_half = heads_data[..., half_dim:]
    cos_part = cos_table[:, None, :]
    sine_part = sine_table[:, None, :]
    return jnp.concatenate(
        [
            first_half * cos_part - second_half * sine_part,
            second_half * cos_part + first_half * sine_part,
        ],
        axis=-1,
    )


def swiglu(gate_pre, up_pre):
    return jax.nn.silu(gate_pre) * up_pre


def contract_rows(left, right):
    return lax.dot_general(
        left, right, (((0,), (0,)), ((), ())), preferred_element_type=jnp.float32
    )


def times_transpose(left, right):
    return lax.dot_general(
        left, right, (((1,), (1,)), ((), ())), preferred_element_type=jnp.float32
    )


def per_device(
    layer_input,
    cotangent,
    segment_ids,
    query_weight,
    key_weight,
    value_weight,
    output_weight,
    gate_weight,
    up_weight,
    down_weight,
    first_gain,
    first_bias,
    second_gain,
    second_bias,
):
    model_width = layer_input.shape[2]
    length = segment_ids.shape[1]
    block_rows = min(512, length)
    block_count = length // block_rows
    local_heads = query_weight.shape[1] // HD
    local_width = local_heads * HD
    score_scale = HD ** (-0.5)
    cos_table, sine_table = rotary_tables(length, HD)

    def fetch_weights():
        row_parts = (
            lax.all_gather(query_weight, "dp", axis=0, tiled=True),
            lax.all_gather(key_weight, "dp", axis=0, tiled=True),
            lax.all_gather(value_weight, "dp", axis=0, tiled=True),
            lax.all_gather(gate_weight, "dp", axis=0, tiled=True),
            lax.all_gather(up_weight, "dp", axis=0, tiled=True),
        )
        col_parts = (
            lax.all_gather(output_weight, "dp", axis=1, tiled=True),
            lax.all_gather(down_weight, "dp", axis=1, tiled=True),
        )
        return tuple(row_parts) + tuple(col_parts)

    def micro_step(weights, row_input, row_cotangent, segment_row):
        query_full, key_full, value_full, gate_full, up_full, output_full, down_full = weights
        full_input = lax.all_gather(row_input, "tensor", axis=0, tiled=True)
        query_pre = jnp.dot(full_input, query_full, preferred_element_type=jnp.float32).reshape(
            length, local_heads, HD
        )
        key_pre = jnp.dot(full_input, key_full, preferred_element_type=jnp.float32).reshape(
            length, local_heads, HD
        )
        value_rows = (
            jnp.dot(full_input, value_full, preferred_element_type=jnp.float32)
            .astype(jnp.bfloat16)
            .reshape(length, local_heads, HD)
        )
        query_rows = rotate(query_pre, cos_table, sine_table).astype(jnp.bfloat16)
        key_rows = rotate(key_pre, cos_table, sine_table).astype(jnp.bfloat16)
        query_blocks = query_rows.reshape(block_count, block_rows, local_heads, HD)
        segment_blocks = segment_row.reshape(block_count, block_rows)

        def block_scores(query_block, segment_block):
            scores = (
                jnp.einsum(
                    "qhd,khd->hqk", query_block, key_rows, preferred_element_type=jnp.float32
                )
                * score_scale
            )
            allowed = segment_block[:, None] == segment_row[None, :]
            return jnp.where(allowed[None, :, :], scores, mask_fill)

        def attend_forward(block_inputs):
            scores = block_scores(block_inputs[0], block_inputs[1])
            row_max = jnp.max(scores, axis=-1, keepdims=True)
            exponent_terms = jnp.exp(scores - row_max)
            row_total = jnp.sum(exponent_terms, axis=-1, keepdims=True)
            probabilities = (exponent_terms / row_total).astype(jnp.bfloat16)
            mixed_rows = jnp.einsum(
                "hqk,khd->qhd", probabilities, value_rows, preferred_element_type=jnp.float32
            )
            return (mixed_rows, (row_max + jnp.log(row_total))[..., 0])

        mixed_blocks, log_totals = lax.map(attend_forward, (query_blocks, segment_blocks))
        attended = mixed_blocks.reshape(length, local_width).astype(jnp.bfloat16)
        attention_branch = lax.psum_scatter(
            jnp.dot(attended, output_full, preferred_element_type=jnp.float32).astype(jnp.bfloat16),
            "tensor",
            scatter_dimension=0,
            tiled=True,
        ).astype(jnp.float32)
        first_sum = row_input.astype(jnp.float32) + attention_branch
        hidden_state, first_back = jax.vjp(layer_norm, first_sum, first_gain, first_bias)
        full_hidden = lax.all_gather(
            hidden_state.astype(jnp.bfloat16), "tensor", axis=0, tiled=True
        )
        gate_pre = jnp.dot(full_hidden, gate_full, preferred_element_type=jnp.float32)
        up_pre = jnp.dot(full_hidden, up_full, preferred_element_type=jnp.float32)
        activated_exact, swiglu_back = jax.vjp(swiglu, gate_pre, up_pre)
        activated = activated_exact.astype(jnp.bfloat16)
        feed_branch = lax.psum_scatter(
            jnp.dot(activated, down_full, preferred_element_type=jnp.float32).astype(jnp.bfloat16),
            "tensor",
            scatter_dimension=0,
            tiled=True,
        ).astype(jnp.float32)
        layer_output, second_back = jax.vjp(
            layer_norm, hidden_state + feed_branch, second_gain, second_bias
        )
        grad_second_sum, grad_second_gain, grad_second_bias = second_back(
            row_cotangent.astype(jnp.float32)
        )
        grad_second_full = lax.all_gather(
            grad_second_sum.astype(jnp.bfloat16), "tensor", axis=0, tiled=True
        )
        grad_activated = times_transpose(grad_second_full, down_full)
        grad_down = contract_rows(activated, grad_second_full)
        grad_gate_pre, grad_up_pre = swiglu_back(grad_activated)
        gate_low = grad_gate_pre.astype(jnp.bfloat16)
        up_low = grad_up_pre.astype(jnp.bfloat16)
        grad_hidden = grad_second_sum + lax.psum_scatter(
            (times_transpose(gate_low, gate_full) + times_transpose(up_low, up_full)).astype(
                jnp.bfloat16
            ),
            "tensor",
            scatter_dimension=0,
            tiled=True,
        ).astype(jnp.float32)
        grad_gate = contract_rows(full_hidden, gate_low)
        grad_up = contract_rows(full_hidden, up_low)
        grad_first_sum, grad_first_gain, grad_first_bias = first_back(grad_hidden)
        grad_first_full = lax.all_gather(
            grad_first_sum.astype(jnp.bfloat16), "tensor", axis=0, tiled=True
        )
        grad_attended = (
            times_transpose(grad_first_full, output_full)
            .astype(jnp.bfloat16)
            .reshape(block_count, block_rows, local_heads, HD)
        )
        grad_output = contract_rows(attended, grad_first_full)

        def attend_backward(sums_carry, block_inputs):
            key_sum, value_sum = sums_carry
            query_block, segment_block, log_block, grad_block = block_inputs
            scores = block_scores(query_block, segment_block)
            probabilities = jnp.exp(scores - log_block[..., None])
            grad_softmax = jnp.einsum(
                "qhd,khd->hqk", grad_block, value_rows, preferred_element_type=jnp.float32
            )
            value_sum = value_sum + jnp.einsum(
                "hqk,qhd->khd",
                probabilities.astype(jnp.bfloat16),
                grad_block,
                preferred_element_type=jnp.float32,
            )
            row_inner = jnp.sum(probabilities * grad_softmax, axis=-1, keepdims=True)
            grad_scores = (probabilities * (grad_softmax - row_inner)).astype(jnp.bfloat16)
            grad_query_block = (
                jnp.einsum(
                    "hqk,khd->qhd", grad_scores, key_rows, preferred_element_type=jnp.float32
                )
                * score_scale
            )
            key_sum = (
                key_sum
                + jnp.einsum(
                    "hqk,qhd->khd", grad_scores, query_block, preferred_element_type=jnp.float32
                )
                * score_scale
            )
            return ((key_sum, value_sum), grad_query_block)

        zero_heads = jnp.zeros((length, local_heads, HD), jnp.float32)
        (grad_key_rot, grad_value_rows), grad_query_blocks = lax.scan(
            attend_backward,
            (zero_heads, zero_heads),
            (query_blocks, segment_blocks, log_totals, grad_attended),
        )
        grad_query_low = (
            rotate(grad_query_blocks.reshape(length, local_heads, HD), cos_table, -sine_table)
            .astype(jnp.bfloat16)
            .reshape(length, local_width)
        )
        grad_key_low = (
            rotate(grad_key_rot, cos_table, -sine_table)
            .astype(jnp.bfloat16)
            .reshape(length, local_width)
        )
        grad_value_low = grad_value_rows.astype(jnp.bfloat16).reshape(length, local_width)
        query_part = times_transpose(grad_query_low, query_full)
        key_part = times_transpose(grad_key_low, key_full)
        value_part = times_transpose(grad_value_low, value_full)
        grad_input = grad_first_sum + lax.psum_scatter(
            (query_part + key_part + value_part).astype(jnp.bfloat16),
            "tensor",
            scatter_dimension=0,
            tiled=True,
        ).astype(jnp.float32)
        row_grads = (
            contract_rows(full_input, grad_query_low),
            contract_rows(full_input, grad_key_low),
            contract_rows(full_input, grad_value_low),
            grad_gate,
            grad_up,
        )
        col_grads = (grad_output, grad_down)
        norm_parts = (grad_first_gain, grad_first_bias, grad_second_gain, grad_second_bias)
        return (
            layer_output.astype(jnp.bfloat16),
            grad_input.astype(jnp.bfloat16),
            (row_grads, col_grads, norm_parts),
        )

    norm_zero = tuple(
        (
            jnp.zeros(gain_like.shape, jnp.float32)
            for gain_like in (first_gain, first_bias, second_gain, second_bias)
        )
    )
    row_zero = tuple(
        (
            jnp.zeros((model_width, weight_part.shape[1]), jnp.float32)
            for weight_part in (query_weight, key_weight, value_weight, gate_weight, up_weight)
        )
    )
    col_zero = (
        jnp.zeros((output_weight.shape[0], model_width), jnp.float32),
        jnp.zeros((down_weight.shape[0], model_width), jnp.float32),
    )

    def scan_step(totals, batch_rows):
        weights = fetch_weights()
        layer_output, grad_input, grad_terms = micro_step(
            weights, batch_rows[0], batch_rows[1], batch_rows[2]
        )
        return (jax.tree.map(jnp.add, totals, grad_terms), (layer_output, grad_input))

    totals, (outputs, grad_inputs) = lax.scan(
        scan_step, (row_zero, col_zero, norm_zero), (layer_input, cotangent, segment_ids)
    )
    row_grads, col_grads, norm_parts = totals
    row_done = lax.psum_scatter(row_grads, "dp", scatter_dimension=0, tiled=True)
    col_done = (
        lax.psum_scatter(col_grads[0], "dp", scatter_dimension=1, tiled=True),
        lax.psum_scatter(col_grads[1], "dp", scatter_dimension=1, tiled=True),
    )
    norm_done = lax.psum(norm_parts, ("dp", "tensor"))
    totals = (tuple(row_done), tuple(col_done), tuple(norm_done))
    row_done, col_done, norm_done = totals
    return (
        outputs,
        grad_inputs,
        row_done[0],
        row_done[1],
        row_done[2],
        col_done[0],
        row_done[3],
        row_done[4],
        col_done[1],
        norm_done[0],
        norm_done[1],
        norm_done[2],
        norm_done[3],
    )


def solution(mesh):
    in_specs = (
        P("dp", "tensor", None),
        P("dp", "tensor", None),
        P("dp", None),
        P("dp", "tensor"),
        P("dp", "tensor"),
        P("dp", "tensor"),
        P("tensor", "dp"),
        P("dp", "tensor"),
        P("dp", "tensor"),
        P("tensor", "dp"),
        P(),
        P(),
        P(),
        P(),
    )
    out_specs = (
        P("dp", "tensor", None),
        P("dp", "tensor", None),
        P("dp", "tensor"),
        P("dp", "tensor"),
        P("dp", "tensor"),
        P("tensor", "dp"),
        P("dp", "tensor"),
        P("dp", "tensor"),
        P("tensor", "dp"),
        P(),
        P(),
        P(),
        P(),
    )
    return jax.shard_map(
        per_device, mesh=mesh, in_specs=in_specs, out_specs=out_specs, check_vma=False
    )
```

profile of v0, /device:TPU:0, one launch (start us, length us, event | category | flops | bytes accessed | tf_op | source)
XLA Modules:
  0.0 1512.0 jit_solution(8653085761068801146)
XLA Ops:
  9.7 1014.8 %while.85 = (s32[]{:T(128)}, f32[768,192]{0,1:T(8,128)}, f32[768,192]{0,1:T(8,128)}, f32[768,192]{0,1:T(8,128)}, f32[768,768]{1,0:T(8,128)}, /*index=5*/f32[768,...) while((s32[]{:T(128)}, f32[768,192]{0,1:T(8,128)}, ...), condition=%wide.region_24.25_spmd.clone.clone.clone.clone, body=%wide.region_0.24_spmd.clone.clone.clone.clone.sunk | while | flops 15999043584 | bytes 421072320 | solution.py:290
  13.5 33.2 %all_gather.98 = bf16[192,768]{0,1:T(8,128)(2,1)S(1)} all-gather(bf16[192,96]{0,1:T(8,128)(2,1)} %get-tuple-element.1606), channel_id=1, replica_groups=mesh['dp'=8,'tensor'=4] {'dp'}, dimensions={1}, use_global_device_ids=true | all-gather | bytes 331776 | tf_op jit(solution)/shard_map/while/body/eval_jaxpr/all_gather | solution.py:91
  46.6 31.4 %all_gather.97 = bf16[768,192]{1,0:T(8,128)(2,1)S(1)} all-gather(bf16[96,192]{1,0:T(8,128)(2,1)} %get-tuple-element.1603), channel_id=1, replica_groups=mesh['dp'=8,'tensor'=4] {'dp'}, dimensions={0}, use_global_device_ids=true | all-gather | bytes 331776 | tf_op jit(solution)/shard_map/while/body/eval_jaxpr/all_gather | solution.py:86
  78.1 31.3 %all_gather.95 = bf16[768,192]{1,0:T(8,128)(2,1)S(1)} all-gather(bf16[96,192]{1,0:T(8,128)(2,1)} %get-tuple-element.1602), channel_id=1, replica_groups=mesh['dp'=8,'tensor'=4] {'dp'}, dimensions={0}, use_global_device_ids=true | all-gather | bytes 331776 | tf_op jit(solution)/shard_map/while/body/eval_jaxpr/all_gather | solution.py:85
  109.4 31.0 %all_gather.96 = bf16[768,192]{1,0:T(8,128)(2,1)S(1)} all-gather(bf16[96,192]{1,0:T(8,128)(2,1)S(1)} %copy-done.33), channel_id=1, replica_groups=mesh['dp'=8,'tensor'=4] {'dp'}, dimensions={0}, use_global_device_ids=true | all-gather | bytes 331776 | tf_op jit(solution)/shard_map/while/body/eval_jaxpr/all_gather | solution.py:84
  161.5 28.5 %reduce-scatter.28.cloned.1.call-done = bf16[256,768]{1,0:T(8,128)(2,1)} async-done(((bf16[1024,768]{1,0:T(8,128)(2,1)}), bf16[256,768]{1,0:T(8,128)(2,1)}) %reduce-scatter.28.cloned.1.call-update) | async-done | bytes 393232 | tf_op jit(solution)/shard_map/while/body/eval_jaxpr/reduce_scatter | solution.py:138
  230.2 39.1 %all-gather.20.cloned.1.call-done = bf16[768,768]{1,0:T(8,128)(2,1)} async-done(((bf16[96,768]{1,0:T(8,128)(2,1)}), bf16[768,768]{1,0:T(8,128)(2,1)}) %all-gather.20.cloned.1.call-update) | async-done | bytes 1179664 | tf_op jit(solution)/shard_map/while/body/eval_jaxpr/all_gather | solution.py:88
  275.7 36.1 %all-gather.22.cloned.1.call-done = bf16[768,768]{0,1:T(8,128)(2,1)} async-done(((bf16[768,96]{0,1:T(8,128)(2,1)}), bf16[768,768]{0,1:T(8,128)(2,1)}) %all-gather.22.cloned.1.call-update) | async-done | bytes 1179664 | tf_op jit(solution)/shard_map/while/body/eval_jaxpr/all_gather | solution.py:92
  438.1 40.8 %while.87 = (s32[]{:T(128)}, f32[1024,3,64]{0,2,1:T(8,128)S(1)}, f32[1024,3,64]{0,2,1:T(8,128)}, f32[2,512,3,64]{1,0,3,2:T(2,128)}, bf16[2,512,3,64]{1,3,2,0:T(8...) while((s32[]{:T(128)}, f32[1024,3,64]{0,2,1:T(8,128)S(1)}, ...), condition=%wide.region_18.18_spmd.clone, body=%wide.region_16.17_spmd.clone.sunk | while | flops 1031830016 | bytes 56418472 | solution.py:226
  521.0 31.5 %all_gather.98 = bf16[192,768]{0,1:T(8,128)(2,1)S(1)} all-gather(bf16[192,96]{0,1:T(8,128)(2,1)} %get-tuple-element.1606), channel_id=1, replica_groups=mesh['dp'=8,'tensor'=4] {'dp'}, dimensions={1}, use_global_device_ids=true | all-gather | bytes 331776 | tf_op jit(solution)/shard_map/while/body/eval_jaxpr/all_gather | solution.py:91
  552.5 31.4 %all_gather.97 = bf16[768,192]{1,0:T(8,128)(2,1)S(1)} all-gather(bf16[96,192]{1,0:T(8,128)(2,1)} %get-tuple-element.1603), channel_id=1, replica_groups=mesh['dp'=8,'tensor'=4] {'dp'}, dimensions={0}, use_global_device_ids=true | all-gather | bytes 331776 | tf_op jit(solution)/shard_map/while/body/eval_jaxpr/all_gather | solution.py:86
  583.9 31.4 %all_gather.95 = bf16[768,192]{1,0:T(8,128)(2,1)S(1)} all-gather(bf16[96,192]{1,0:T(8,128)(2,1)} %get-tuple-element.1602), channel_id=1, replica_groups=mesh['dp'=8,'tensor'=4] {'dp'}, dimensions={0}, use_global_device_ids=true | all-gather | bytes 331776 | tf_op jit(solution)/shard_map/while/body/eval_jaxpr/all_gather | solution.py:85
  615.3 31.0 %all_gather.96 = bf16[768,192]{1,0:T(8,128)(2,1)S(1)} all-gather(bf16[96,192]{1,0:T(8,128)(2,1)S(1)} %copy-done.33), channel_id=1, replica_groups=mesh['dp'=8,'tensor'=4] {'dp'}, dimensions={0}, use_global_device_ids=true | all-gather | bytes 331776 | tf_op jit(solution)/shard_map/while/body/eval_jaxpr/all_gather | solution.py:84
  735.1 39.1 %all-gather.20.cloned.1.call-done = bf16[768,768]{1,0:T(8,128)(2,1)} async-done(((bf16[96,768]{1,0:T(8,128)(2,1)}), bf16[768,768]{1,0:T(8,128)(2,1)}) %all-gather.20.cloned.1.call-update) | async-done | bytes 1179664 | tf_op jit(solution)/shard_map/while/body/eval_jaxpr/all_gather | solution.py:88
  780.6 36.1 %all-gather.22.cloned.1.call-done = bf16[768,768]{0,1:T(8,128)(2,1)} async-done(((bf16[768,96]{0,1:T(8,128)(2,1)}), bf16[768,768]{0,1:T(8,128)(2,1)}) %all-gather.22.cloned.1.call-update) | async-done | bytes 1179664 | tf_op jit(solution)/shard_map/while/body/eval_jaxpr/all_gather | solution.py:92
  884.7 28.3 %reduce-scatter.32.cloned.1.call-done = bf16[256,768]{1,0:T(8,128)(2,1)} async-done(((bf16[1024,768]{1,0:T(8,128)(2,1)}), bf16[256,768]{1,0:T(8,128)(2,1)}) %reduce-scatter.32.cloned.1.call-update) | async-done | bytes 393232 | tf_op jit(solution)/shard_map/while/body/eval_jaxpr/reduce_scatter | solution.py:173
  943.0 40.5 %while.87 = (s32[]{:T(128)}, f32[1024,3,64]{0,2,1:T(8,128)S(1)}, f32[1024,3,64]{0,2,1:T(8,128)}, f32[2,512,3,64]{1,0,3,2:T(2,128)}, bf16[2,512,3,64]{1,3,2,0:T(8...) while((s32[]{:T(128)}, f32[1024,3,64]{0,2,1:T(8,128)S(1)}, ...), condition=%wide.region_18.18_spmd.clone, body=%wide.region_16.17_spmd.clone.sunk | while | flops 1031830016 | bytes 56418472 | solution.py:226
  1036.1 39.7 %all-reduce = (f32[768]{0:T(1024)}, f32[768]{0:T(1024)}, f32[768]{0:T(1024)}, f32[768]{0:T(1024)}) all-reduce(f32[768]{0:T(1024)S(1)} %copy-done.58, f32[768]{0:T(1024)S(1)} %copy-done.55, f32[768]{0:T(1024)S(1)} %copy-done.52, f32[768]{0:T(1024)S(1)} %copy-done.49), channel_id=1, replica_groups=mesh['dp'=8,'tensor'=4] {'dp','tensor'}, use_global_device_ids=true, to_apply=%region_32.33 | all-reduce | flops 3072 | bytes 24576 | tf_op jit(solution)/shard_map/psum | solution.py:299
  1092.5 64.2 %reduce-scatter.14.cloned.1.call-done = f32[96,192]{1,0:T(8,128)} async-done(((f32[768,192]{1,0:T(8,128)}), f32[96,192]{1,0:T(8,128)}) %reduce-scatter.14.cloned.1.call-update) | async-done | bytes 73744 | tf_op jit(solution)/shard_map/reduce_scatter | solution.py:294
  1156.7 65.5 %reduce-scatter.16.cloned.1.call-done = f32[96,192]{1,0:T(8,128)} async-done(((f32[768,192]{1,0:T(8,128)}), f32[96,192]{1,0:T(8,128)}) %reduce-scatter.16.cloned.1.call-update) | async-done | bytes 73744 | tf_op jit(solution)/shard_map/reduce_scatter | solution.py:294
  1222.2 65.8 %reduce-scatter.18.cloned.1.call-done = f32[96,192]{1,0:T(8,128)} async-done(((f32[768,192]{1,0:T(8,128)}), f32[96,192]{1,0:T(8,128)}) %reduce-scatter.18.cloned.1.call-update) | async-done | bytes 73744 | tf_op jit(solution)/shard_map/reduce_scatter | solution.py:294
  1288.0 72.2 %reduce-scatter.20.cloned.1.call-done = f32[96,768]{1,0:T(8,128)} async-done(((f32[768,768]{1,0:T(8,128)}), f32[96,768]{1,0:T(8,128)}) %reduce-scatter.20.cloned.1.call-update) | async-done | bytes 294928 | tf_op jit(solution)/shard_map/reduce_scatter | solution.py:294
  1360.1 72.1 %reduce-scatter.22.cloned.1.call-done = f32[96,768]{1,0:T(8,128)} async-done(((f32[768,768]{1,0:T(8,128)}), f32[96,768]{1,0:T(8,128)}) %reduce-scatter.22.cloned.1.call-update) | async-done | bytes 294928 | tf_op jit(solution)/shard_map/reduce_scatter | solution.py:294
  1432.2 72.0 %reduce-scatter.24.cloned.1.call-done = f32[768,96]{0,1:T(8,128)} async-done(((f32[768,768]{0,1:T(8,128)}), f32[768,96]{0,1:T(8,128)}) %reduce-scatter.24.cloned.1.call-update) | async-done | bytes 294928 | tf_op jit(solution)/shard_map/reduce_scatter | solution.py:297
  (566 shorter events, 604.8 us)
Async XLA Ops:
  9.7 131.9 %all-gather.14.cloned.1.call-start = ((), (), s32[]{:S(2)}) async-start(), calls=%async_computation.18 | async-start | bytes 1966080 | tf_op jit(solution)/shard_map/while/body/eval_jaxpr/all_gather | solution.py:98
  11.5 178.5 %reduce-scatter.28.cloned.1.call-start = ((), (), s32[]{:S(2)}) async-start(), calls=%async_computation.19 | async-start | bytes 1966080 | tf_op jit(solution)/shard_map/while/body/eval_jaxpr/reduce_scatter | solution.py:138
  161.4 64.0 %all-gather.16.cloned.1.call-start = ((), (), s32[]{:S(2)}) async-start(), calls=%async_computation.20 | async-start | bytes 1966080 | tf_op jit(solution)/shard_map/while/body/eval_jaxpr/all_gather | solution.py:146
  194.5 74.7 %all-gather.20.cloned.1.call-start = ((), (), s32[]{:S(2)}) async-start(), calls=%async_computation.22 | async-start | bytes 1327104 | tf_op jit(solution)/shard_map/while/body/eval_jaxpr/all_gather | solution.py:88
  195.1 116.6 %all-gather.22.cloned.1.call-start = ((), (), s32[]{:S(2)}) async-start(), calls=%async_computation.23 | async-start | bytes 1327104 | tf_op jit(solution)/shard_map/while/body/eval_jaxpr/all_gather | solution.py:92
  195.9 147.1 %reduce-scatter.30.cloned.1.call-start = ((), (), s32[]{:S(2)}) async-start(), calls=%async_computation.24 | async-start | bytes 1966080 | tf_op jit(solution)/shard_map/while/body/eval_jaxpr/reduce_scatter | solution.py:153
  349.4 58.6 %reduce-scatter.32.cloned.1.call-start = ((), (), s32[]{:S(2)}) async-start(), calls=%async_computation.26 | async-start | bytes 1966080 | tf_op jit(solution)/shard_map/while/body/eval_jaxpr/reduce_scatter | solution.py:173
  379.7 54.2 %all-gather.26.cloned.1.call-start = ((), (), s32[]{:S(2)}) async-start(), calls=%async_computation.27 | async-start | bytes 1966080 | tf_op jit(solution)/shard_map/while/body/eval_jaxpr/all_gather | solution.py:184
  414.3 100.8 %reduce-scatter.34.cloned.1.call-start = ((), (), s32[]{:S(2)}) async-start(), calls=%async_computation.28 | async-start | bytes 1966080 | tf_op jit(solution)/shard_map/while/body/eval_jaxpr/reduce_scatter | solution.py:245
  517.2 130.3 %all-gather.14.cloned.1.call-start = ((), (), s32[]{:S(2)}) async-start(), calls=%async_computation.18 | async-start | bytes 1966080 | tf_op jit(solution)/shard_map/while/body/eval_jaxpr/all_gather | solution.py:98
  519.1 175.9 %reduce-scatter.28.cloned.1.call-start = ((), (), s32[]{:S(2)}) async-start(), calls=%async_computation.19 | async-start | bytes 1966080 | tf_op jit(solution)/shard_map/while/body/eval_jaxpr/reduce_scatter | solution.py:138
  667.4 62.9 %all-gather.16.cloned.1.call-start = ((), (), s32[]{:S(2)}) async-start(), calls=%async_computation.20 | async-start | bytes 1966080 | tf_op jit(solution)/shard_map/while/body/eval_jaxpr/all_gather | solution.py:146
  699.5 74.7 %all-gather.20.cloned.1.call-start = ((), (), s32[]{:S(2)}) async-start(), calls=%async_computation.22 | async-start | bytes 1327104 | tf_op jit(solution)/shard_map/while/body/eval_jaxpr/all_gather | solution.py:88
  700.1 116.6 %all-gather.22.cloned.1.call-start = ((), (), s32[]{:S(2)}) async-start(), calls=%async_computation.23 | async-start | bytes 1327104 | tf_op jit(solution)/shard_map/while/body/eval_jaxpr/all_gather | solution.py:92
  700.8 147.1 %reduce-scatter.30.cloned.1.call-start = ((), (), s32[]{:S(2)}) async-start(), calls=%async_computation.24 | async-start | bytes 1966080 | tf_op jit(solution)/shard_map/while/body/eval_jaxpr/reduce_scatter | solution.py:153
  854.4 58.6 %reduce-scatter.32.cloned.1.call-start = ((), (), s32[]{:S(2)}) async-start(), calls=%async_computation.26 | async-start | bytes 1966080 | tf_op jit(solution)/shard_map/while/body/eval_jaxpr/reduce_scatter | solution.py:173
  919.3 100.6 %reduce-scatter.34.cloned.1.call-start = ((), (), s32[]{:S(2)}) async-start(), calls=%async_computation.28 | async-start | bytes 1966080 | tf_op jit(solution)/shard_map/while/body/eval_jaxpr/reduce_scatter | solution.py:245
  1024.5 66.3 %reduce-scatter.26.cloned.1.call-start = ((), (), s32[]{:S(2)}) async-start(), calls=%async_computation.17 | async-start | bytes 884736
  1026.9 129.8 %reduce-scatter.14.cloned.1.call-start = ((), (), s32[]{:S(2)}) async-start(), calls=%async_computation.11 | async-start | bytes 884736 | tf_op jit(solution)/shard_map/reduce_scatter | solution.py:294
  1029.2 193.0 %reduce-scatter.16.cloned.1.call-start = ((), (), s32[]{:S(2)}) async-start(), calls=%async_computation.12 | async-start | bytes 884736 | tf_op jit(solution)/shard_map/reduce_scatter | solution.py:294
  1030.5 257.5 %reduce-scatter.18.cloned.1.call-start = ((), (), s32[]{:S(2)}) async-start(), calls=%async_computation.13 | async-start | bytes 884736 | tf_op jit(solution)/shard_map/reduce_scatter | solution.py:294
  1031.7 328.4 %reduce-scatter.20.cloned.1.call-start = ((), (), s32[]{:S(2)}) async-start(), calls=%async_computation.14 | async-start | bytes 2654208 | tf_op jit(solution)/shard_map/reduce_scatter | solution.py:294
  1032.5 399.7 %reduce-scatter.22.cloned.1.call-start = ((), (), s32[]{:S(2)}) async-start(), calls=%async_computation.15 | async-start | bytes 2654208 | tf_op jit(solution)/shard_map/reduce_scatter | solution.py:294
  1033.2 470.9 %reduce-scatter.24.cloned.1.call-start = ((), (), s32[]{:S(2)}) async-start(), calls=%async_computation.16 | async-start | bytes 2654208 | tf_op jit(solution)/shard_map/reduce_scatter | solution.py:297
  (136 other events, 1879.1 us)
Sparse Core Ops, SparseCore 0:
  12.1 22.3 all-gather.13
  161.0 29.0 reduce-scatter.27
  316.3 26.6 reduce-scatter.29
  379.8 28.1 reduce-scatter.31
  486.9 28.1 reduce-scatter.33
  519.3 19.6 all-gather.13
  666.9 28.0 reduce-scatter.27
  821.2 26.6 reduce-scatter.29
  884.8 28.1 reduce-scatter.31
  991.6 28.1 reduce-scatter.33
Sparse Core Ops, SparseCore 1:
  163.5 42.3 all-gather.17
  207.4 18.0 all-gather.15
  227.7 41.5 all-gather.19
  271.7 40.0 all-gather.21
  349.5 19.5 all-gather.23
  414.4 19.5 all-gather.25
  669.5 41.3 all-gather.17
  712.4 17.9 all-gather.15
  732.6 41.5 all-gather.19
  776.6 40.0 all-gather.21
  854.5 19.5 all-gather.23
  919.3 19.5 all-gather.25
  1028.3 62.5 reduce-scatter.25
  1095.1 61.5 reduce-scatter.13
  1160.6 61.5 reduce-scatter.15
  1226.4 61.5 reduce-scatter.17
  1292.1 68.0 reduce-scatter.19
  1364.2 67.9 reduce-scatter.21
  1436.1 68.0 reduce-scatter.23
where the time goes:
time: 1520 us; the launch traced here: 1510 us
  waiting for transfers between devices  898 us (59%)
  blocking collectives  292 us (19%)
  matrix products  147 us (10%)
  local copies, waits for them, and re-layouts  78.3 us (5%)
  other arithmetic  72.1 us (5%)
  between operations  16.2 us (1%)
    reduce_scatter x5, waiting for transfers between devices, per_device(): lax.psum_scatter(row_grads, 'dp', scatter_dimension=0, tiled=True)  340 us
    all_gather x2, waiting for transfers between devices, fetch_weights(): lax.all_gather(up_weight, 'dp', axis=0, tiled=True)  78.1 us
    all_gather x2, waiting for transfers between devices, fetch_weights(): lax.all_gather(down_weight, 'dp', axis=1, tiled=True)  72.2 us
    reduce_scatter x1, waiting for transfers between devices, per_device(): lax.psum_scatter(col_grads[1], 'dp', scatter_dimension=1, tiled=True)  72 us
    all_gather x2, blocking collectives, fetch_weights(): lax.all_gather(output_weight, 'dp', axis=1, tiled=True)  64.6 us
    all_gather x2, blocking collectives, fetch_weights(): lax.all_gather(value_weight, 'dp', axis=0, tiled=True)  62.8 us
    all_gather x2, blocking collectives, fetch_weights(): lax.all_gather(key_weight, 'dp', axis=0, tiled=True)  62.8 us
    all_gather x2, blocking collectives, fetch_weights(): lax.all_gather(query_weight, 'dp', axis=0, tiled=True)  61.9 us
  transfers between devices with their start and end apart: 29, of which 27 were waited for; matrix products, arithmetic and copies ran while one was open for 5% of the time, Pallas kernels for 0%

commit v1 on v0

--- a/solution.py
+++ b/solution.py
@@ -7,6 +7,28 @@
 eps_norm = 1e-06
 rope_base = 1000.0
 mask_fill = -1e30
+
+
+def joined_along(pieces, dim):
+    shape = list(pieces.shape[1:])
+    shape[dim] *= pieces.shape[0]
+    return jnp.moveaxis(pieces, 0, dim).reshape(shape)
+
+
+def collected_by_bits(value, axis):
+    length = lax.axis_size(axis)
+    blocks = value[None]
+    for level in range(length.bit_length() - 1):
+        bit = 1 << level
+        other = lax.ppermute(blocks, axis, [(i, i ^ bit) for i in range(length)])
+        both = jnp.stack([blocks, other])
+        upper = lax.axis_index(axis) >> level & 1
+        blocks = jnp.where(upper == 0, both, both[::-1]).reshape(-1, *value.shape)
+    return blocks
+
+
+def doubled_up(value, axis, dim):
+    return joined_along(collected_by_bits(value, axis), dim)
 
 
 def layer_norm(field_rows, gain_vec, bias_vec):
@@ -82,7 +104,7 @@
     def fetch_weights():
         row_parts = (
             lax.all_gather(query_weight, "dp", axis=0, tiled=True),
-            lax.all_gather(key_weight, "dp", axis=0, tiled=True),
+            doubled_up(key_weight, "dp", 0),
             lax.all_gather(value_weight, "dp", axis=0, tiled=True),
             lax.all_gather(gate_weight, "dp", axis=0, tiled=True),
             lax.all_gather(up_weight, "dp", axis=0, tiled=True),

time: 1520 us -> 1460 us (0.961)
  blocking collectives: 292 us -> 228 us
    all_gather x2 -> x0, blocking collectives: 62.8 us -> none  [fetch_weights(): lax.all_gather(key_weight, 'dp', axis=0, tiled=True)]
  transfers between devices with their start and end apart: 29 -> 34, of which waited for: 27 -> 28; matrix products, arithmetic and copies ran while one was open for 5% -> 5% of each run, Pallas kernels for 0% -> 0%
where the time goes in v1:
time: 1460 us; the launch traced here: 1450 us
  waiting for transfers between devices  900 us (62%)
  blocking collectives  228 us (16%)
  matrix products  144 us (10%)
  local copies, waits for them, and re-layouts  79.1 us (5%)
  other arithmetic  70.9 us (5%)
  between operations  16.2 us (1%)
    reduce_scatter x5, waiting for transfers between devices, per_device(): lax.psum_scatter(row_grads, 'dp', scatter_dimension=0, tiled=True)  340 us
    all_gather x2, waiting for transfers between devices, fetch_weights(): lax.all_gather(up_weight, 'dp', axis=0, tiled=True)  78.2 us
    all_gather x2, waiting for transfers between devices, fetch_weights(): lax.all_gather(down_weight, 'dp', axis=1, tiled=True)  72.1 us
    reduce_scatter x1, waiting for transfers between devices, per_device(): lax.psum_scatter(col_grads[1], 'dp', scatter_dimension=1, tiled=True)  72 us
    all_gather x2, blocking collectives, fetch_weights(): lax.all_gather(value_weight, 'dp', axis=0, tiled=True)  63.2 us
    all_gather x2, blocking collectives, fetch_weights(): lax.all_gather(output_weight, 'dp', axis=1, tiled=True)  62.9 us
    all_gather x2, blocking collectives, fetch_weights(): lax.all_gather(query_weight, 'dp', axis=0, tiled=True)  62 us
    reduce_scatter x2, waiting for transfers between devices, micro_step(): lax.psum_scatter((times_transpose(gate_low, gate_full) + times_transpose(...  56.5 us
  transfers between devices with their start and end apart: 34, of which 28 were waited for; matrix products, arithmetic and copies ran while one was open for 5% of the time, Pallas kernels for 0%

profile of v1, /device:TPU:0, one launch (start us, length us, event | category | flops | bytes accessed | tf_op | source)
XLA Modules:
  0.0 1453.5 jit_solution(3627215957472515313)
XLA Ops:
  14.8 951.0 %while.95 = (s32[]{:T(128)}, f32[768,192]{0,1:T(8,128)}, f32[768,192]{0,1:T(8,128)}, f32[768,192]{0,1:T(8,128)}, f32[768,768]{1,0:T(8,128)}, /*index=5*/f32[768,...) while((s32[]{:T(128)}, f32[768,192]{0,1:T(8,128)}, ...), condition=%wide.region_24.25_spmd.clone.clone.clone.clone, body=%wide.region_0.24_spmd.clone.clone.clone.clone.sunk | while | flops 15999522816 | bytes 433993472 | solution.py:312
  19.9 31.5 %all_gather.98 = bf16[192,768]{0,1:T(8,128)(2,1)S(1)} all-gather(bf16[192,96]{0,1:T(8,128)(2,1)} %get-tuple-element.1705), channel_id=1, replica_groups=mesh['dp'=8,'tensor'=4] {'dp'}, dimensions={1}, use_global_device_ids=true | all-gather | bytes 331776 | tf_op jit(solution)/shard_map/while/body/eval_jaxpr/all_gather | solution.py:113
  52.0 31.6 %all_gather.97 = bf16[768,192]{1,0:T(8,128)(2,1)S(1)} all-gather(bf16[96,192]{1,0:T(8,128)(2,1)} %get-tuple-element.1702), channel_id=1, replica_groups=mesh['dp'=8,'tensor'=4] {'dp'}, dimensions={0}, use_global_device_ids=true | all-gather | bytes 331776 | tf_op jit(solution)/shard_map/while/body/eval_jaxpr/all_gather | solution.py:108
  85.0 31.1 %all_gather.96 = bf16[768,192]{1,0:T(8,128)(2,1)S(1)} all-gather(bf16[96,192]{1,0:T(8,128)(2,1)S(1)} %copy-done.36), channel_id=1, replica_groups=mesh['dp'=8,'tensor'=4] {'dp'}, dimensions={0}, use_global_device_ids=true | all-gather | bytes 331776 | tf_op jit(solution)/shard_map/while/body/eval_jaxpr/all_gather | solution.py:106
  135.2 27.3 %reduce-scatter.28.cloned.1.call-done = bf16[256,768]{1,0:T(8,128)(2,1)} async-done(((bf16[1024,768]{1,0:T(8,128)(2,1)}), bf16[256,768]{1,0:T(8,128)(2,1)}) %reduce-scatter.28.cloned.1.call-update) | async-done | bytes 393232 | tf_op jit(solution)/shard_map/while/body/eval_jaxpr/reduce_scatter | solution.py:160
  202.6 39.1 %all-gather.20.cloned.1.call-done = bf16[768,768]{1,0:T(8,128)(2,1)} async-done(((bf16[96,768]{1,0:T(8,128)(2,1)}), bf16[768,768]{1,0:T(8,128)(2,1)}) %all-gather.20.cloned.1.call-update) | async-done | bytes 1179664 | tf_op jit(solution)/shard_map/while/body/eval_jaxpr/all_gather | solution.py:110
  248.1 36.0 %all-gather.22.cloned.1.call-done = bf16[768,768]{0,1:T(8,128)(2,1)} async-done(((bf16[768,96]{0,1:T(8,128)(2,1)}), bf16[768,768]{0,1:T(8,128)(2,1)}) %all-gather.22.cloned.1.call-update) | async-done | bytes 1179664 | tf_op jit(solution)/shard_map/while/body/eval_jaxpr/all_gather | solution.py:114
  352.1 28.3 %reduce-scatter.32.cloned.1.call-done = bf16[256,768]{1,0:T(8,128)(2,1)} async-done(((bf16[1024,768]{1,0:T(8,128)(2,1)}), bf16[256,768]{1,0:T(8,128)(2,1)}) %reduce-scatter.32.cloned.1.call-update) | async-done | bytes 393232 | tf_op jit(solution)/shard_map/while/body/eval_jaxpr/reduce_scatter | solution.py:195
  410.5 40.8 %while.97 = (s32[]{:T(128)}, f32[1024,3,64]{0,2,1:T(8,128)S(1)}, f32[1024,3,64]{0,2,1:T(8,128)}, f32[2,512,3,64]{1,0,3,2:T(2,128)}, bf16[2,512,3,64]{1,3,2,0:T(8...) while((s32[]{:T(128)}, f32[1024,3,64]{0,2,1:T(8,128)S(1)}, ...), condition=%wide.region_18.18_spmd.clone, body=%wide.region_16.17_spmd.clone.sunk | while | flops 1031830016 | bytes 56418472 | solution.py:248
  494.3 31.3 %all_gather.98 = bf16[192,768]{0,1:T(8,128)(2,1)S(1)} all-gather(bf16[192,96]{0,1:T(8,128)(2,1)} %get-tuple-element.1705), channel_id=1, replica_groups=mesh['dp'=8,'tensor'=4] {'dp'}, dimensions={1}, use_global_device_ids=true | all-gather | bytes 331776 | tf_op jit(solution)/shard_map/while/body/eval_jaxpr/all_gather | solution.py:113
  526.1 31.5 %all_gather.97 = bf16[768,192]{1,0:T(8,128)(2,1)S(1)} all-gather(bf16[96,192]{1,0:T(8,128)(2,1)} %get-tuple-element.1702), channel_id=1, replica_groups=mesh['dp'=8,'tensor'=4] {'dp'}, dimensions={0}, use_global_device_ids=true | all-gather | bytes 331776 | tf_op jit(solution)/shard_map/while/body/eval_jaxpr/all_gather | solution.py:108
  559.1 31.0 %all_gather.96 = bf16[768,192]{1,0:T(8,128)(2,1)S(1)} all-gather(bf16[96,192]{1,0:T(8,128)(2,1)S(1)} %copy-done.36), channel_id=1, replica_groups=mesh['dp'=8,'tensor'=4] {'dp'}, dimensions={0}, use_global_device_ids=true | all-gather | bytes 331776 | tf_op jit(solution)/shard_map/while/body/eval_jaxpr/all_gather | solution.py:106
  609.2 27.0 %reduce-scatter.28.cloned.1.call-done = bf16[256,768]{1,0:T(8,128)(2,1)} async-done(((bf16[1024,768]{1,0:T(8,128)(2,1)}), bf16[256,768]{1,0:T(8,128)(2,1)}) %reduce-scatter.28.cloned.1.call-update) | async-done | bytes 393232 | tf_op jit(solution)/shard_map/while/body/eval_jaxpr/reduce_scatter | solution.py:160
  676.3 39.1 %all-gather.20.cloned.1.call-done = bf16[768,768]{1,0:T(8,128)(2,1)} async-done(((bf16[96,768]{1,0:T(8,128)(2,1)}), bf16[768,768]{1,0:T(8,128)(2,1)}) %all-gather.20.cloned.1.call-update) | async-done | bytes 1179664 | tf_op jit(solution)/shard_map/while/body/eval_jaxpr/all_gather | solution.py:110
  721.8 36.0 %all-gather.22.cloned.1.call-done = bf16[768,768]{0,1:T(8,128)(2,1)} async-done(((bf16[768,96]{0,1:T(8,128)(2,1)}), bf16[768,768]{0,1:T(8,128)(2,1)}) %all-gather.22.cloned.1.call-update) | async-done | bytes 1179664 | tf_op jit(solution)/shard_map/while/body/eval_jaxpr/all_gather | solution.py:114
  825.8 28.3 %reduce-scatter.32.cloned.1.call-done = bf16[256,768]{1,0:T(8,128)(2,1)} async-done(((bf16[1024,768]{1,0:T(8,128)(2,1)}), bf16[256,768]{1,0:T(8,128)(2,1)}) %reduce-scatter.32.cloned.1.call-update) | async-done | bytes 393232 | tf_op jit(solution)/shard_map/while/body/eval_jaxpr/reduce_scatter | solution.py:195
  884.2 40.6 %while.97 = (s32[]{:T(128)}, f32[1024,3,64]{0,2,1:T(8,128)S(1)}, f32[1024,3,64]{0,2,1:T(8,128)}, f32[2,512,3,64]{1,0,3,2:T(2,128)}, bf16[2,512,3,64]{1,3,2,0:T(8...) while((s32[]{:T(128)}, f32[1024,3,64]{0,2,1:T(8,128)S(1)}, ...), condition=%wide.region_18.18_spmd.clone, body=%wide.region_16.17_spmd.clone.sunk | while | flops 1031830016 | bytes 56418472 | solution.py:248
  976.4 39.7 %all-reduce = (f32[768]{0:T(1024)}, f32[768]{0:T(1024)}, f32[768]{0:T(1024)}, f32[768]{0:T(1024)}) all-reduce(f32[768]{0:T(1024)S(1)} %copy-done.61, f32[768]{0:T(1024)S(1)} %copy-done.58, f32[768]{0:T(1024)S(1)} %copy-done.55, f32[768]{0:T(1024)S(1)} %copy-done.52), channel_id=1, replica_groups=mesh['dp'=8,'tensor'=4] {'dp','tensor'}, use_global_device_ids=true, to_apply=%region_32.33 | all-reduce | flops 3072 | bytes 24576 | tf_op jit(solution)/shard_map/psum | solution.py:321
  1033.9 64.2 %reduce-scatter.14.cloned.1.call-done = f32[96,192]{1,0:T(8,128)} async-done(((f32[768,192]{1,0:T(8,128)}), f32[96,192]{1,0:T(8,128)}) %reduce-scatter.14.cloned.1.call-update) | async-done | bytes 73744 | tf_op jit(solution)/shard_map/reduce_scatter | solution.py:316
  1098.1 65.5 %reduce-scatter.16.cloned.1.call-done = f32[96,192]{1,0:T(8,128)} async-done(((f32[768,192]{1,0:T(8,128)}), f32[96,192]{1,0:T(8,128)}) %reduce-scatter.16.cloned.1.call-update) | async-done | bytes 73744 | tf_op jit(solution)/shard_map/reduce_scatter | solution.py:316
  1163.6 65.9 %reduce-scatter.18.cloned.1.call-done = f32[96,192]{1,0:T(8,128)} async-done(((f32[768,192]{1,0:T(8,128)}), f32[96,192]{1,0:T(8,128)}) %reduce-scatter.18.cloned.1.call-update) | async-done | bytes 73744 | tf_op jit(solution)/shard_map/reduce_scatter | solution.py:316
  1229.5 72.1 %reduce-scatter.20.cloned.1.call-done = f32[96,768]{1,0:T(8,128)} async-done(((f32[768,768]{1,0:T(8,128)}), f32[96,768]{1,0:T(8,128)}) %reduce-scatter.20.cloned.1.call-update) | async-done | bytes 294928 | tf_op jit(solution)/shard_map/reduce_scatter | solution.py:316
  1301.6 72.1 %reduce-scatter.22.cloned.1.call-done = f32[96,768]{1,0:T(8,128)} async-done(((f32[768,768]{1,0:T(8,128)}), f32[96,768]{1,0:T(8,128)}) %reduce-scatter.22.cloned.1.call-update) | async-done | bytes 294928 | tf_op jit(solution)/shard_map/reduce_scatter | solution.py:316
  1373.7 72.0 %reduce-scatter.24.cloned.1.call-done = f32[768,96]{0,1:T(8,128)} async-done(((f32[768,768]{0,1:T(8,128)}), f32[768,96]{0,1:T(8,128)}) %reduce-scatter.24.cloned.1.call-update) | async-done | bytes 294928 | tf_op jit(solution)/shard_map/reduce_scatter | solution.py:319
  (613 shorter events, 553.5 us)
Async XLA Ops:
  14.8 101.6 %all-gather.14.cloned.1.call-start = ((), (), s32[]{:S(2)}) async-start(), calls=%async_computation.18 | async-start | bytes 1966080 | tf_op jit(solution)/shard_map/while/body/eval_jaxpr/all_gather | solution.py:120
  16.6 145.9 %reduce-scatter.28.cloned.1.call-start = ((), (), s32[]{:S(2)}) async-start(), calls=%async_computation.19 | async-start | bytes 1966080 | tf_op jit(solution)/shard_map/while/body/eval_jaxpr/reduce_scatter | solution.py:160
  17.7 65.9 %collective-permute-start = (bf16[2,96,192]{2,1,0:T(8,128)(2,1)S(1)}, bf16[2,96,192]{2,1,0:T(8,128)(2,1)S(1)}, u32[]{:S(2)}, u32[]{:S(2)}) collective-permute-start(bf16[2,96,192]{2,1,0:T(8,128)(2,1)S(1)} %get-tuple-element.1484), channel_id=1, source_target_pairs={{0,8},{4,12},{8,0},{12,4},{16,24},{20,28},{24,16},{28,20},{1,9},{5... | collective-permute-start | bytes 221192 | tf_op jit(solution)/shard_map/while/body/eval_jaxpr/ppermute | solution.py:23
  135.1 62.7 %all-gather.16.cloned.1.call-start = ((), (), s32[]{:S(2)}) async-start(), calls=%async_computation.20 | async-start | bytes 1966080 | tf_op jit(solution)/shard_map/while/body/eval_jaxpr/all_gather | solution.py:168
  167.0 74.7 %all-gather.20.cloned.1.call-start = ((), (), s32[]{:S(2)}) async-start(), calls=%async_computation.22 | async-start | bytes 1327104 | tf_op jit(solution)/shard_map/while/body/eval_jaxpr/all_gather | solution.py:110
  167.6 116.6 %all-gather.22.cloned.1.call-start = ((), (), s32[]{:S(2)}) async-start(), calls=%async_computation.23 | async-start | bytes 1327104 | tf_op jit(solution)/shard_map/while/body/eval_jaxpr/all_gather | solution.py:114
  168.3 147.0 %reduce-scatter.30.cloned.1.call-start = ((), (), s32[]{:S(2)}) async-start(), calls=%async_computation.24 | async-start | bytes 1966080 | tf_op jit(solution)/shard_map/while/body/eval_jaxpr/reduce_scatter | solution.py:175
  321.8 58.6 %reduce-scatter.32.cloned.1.call-start = ((), (), s32[]{:S(2)}) async-start(), calls=%async_computation.26 | async-start | bytes 1966080 | tf_op jit(solution)/shard_map/while/body/eval_jaxpr/reduce_scatter | solution.py:195
  386.7 101.0 %reduce-scatter.34.cloned.1.call-start = ((), (), s32[]{:S(2)}) async-start(), calls=%async_computation.28 | async-start | bytes 1966080 | tf_op jit(solution)/shard_map/while/body/eval_jaxpr/reduce_scatter | solution.py:267
  489.8 100.6 %all-gather.14.cloned.1.call-start = ((), (), s32[]{:S(2)}) async-start(), calls=%async_computation.18 | async-start | bytes 1966080 | tf_op jit(solution)/shard_map/while/body/eval_jaxpr/all_gather | solution.py:120
  491.7 144.5 %reduce-scatter.28.cloned.1.call-start = ((), (), s32[]{:S(2)}) async-start(), calls=%async_computation.19 | async-start | bytes 1966080 | tf_op jit(solution)/shard_map/while/body/eval_jaxpr/reduce_scatter | solution.py:160
  492.7 65.0 %collective-permute-start = (bf16[2,96,192]{2,1,0:T(8,128)(2,1)S(1)}, bf16[2,96,192]{2,1,0:T(8,128)(2,1)S(1)}, u32[]{:S(2)}, u32[]{:S(2)}) collective-permute-start(bf16[2,96,192]{2,1,0:T(8,128)(2,1)S(1)} %get-tuple-element.1484), channel_id=1, source_target_pairs={{0,8},{4,12},{8,0},{12,4},{16,24},{20,28},{24,16},{28,20},{1,9},{5... | collective-permute-start | bytes 221192 | tf_op jit(solution)/shard_map/while/body/eval_jaxpr/ppermute | solution.py:23
  609.1 62.4 %all-gather.16.cloned.1.call-start = ((), (), s32[]{:S(2)}) async-start(), calls=%async_computation.20 | async-start | bytes 1966080 | tf_op jit(solution)/shard_map/while/body/eval_jaxpr/all_gather | solution.py:168
  640.7 74.7 %all-gather.20.cloned.1.call-start = ((), (), s32[]{:S(2)}) async-start(), calls=%async_computation.22 | async-start | bytes 1327104 | tf_op jit(solution)/shard_map/while/body/eval_jaxpr/all_gather | solution.py:110
  641.3 116.6 %all-gather.22.cloned.1.call-start = ((), (), s32[]{:S(2)}) async-start(), calls=%async_computation.23 | async-start | bytes 1327104 | tf_op jit(solution)/shard_map/while/body/eval_jaxpr/all_gather | solution.py:114
  642.0 147.1 %reduce-scatter.30.cloned.1.call-start = ((), (), s32[]{:S(2)}) async-start(), calls=%async_computation.24 | async-start | bytes 1966080 | tf_op jit(solution)/shard_map/while/body/eval_jaxpr/reduce_scatter | solution.py:175
  860.4 100.7 %reduce-scatter.34.cloned.1.call-start = ((), (), s32[]{:S(2)}) async-start(), calls=%async_computation.28 | async-start | bytes 1966080 | tf_op jit(solution)/shard_map/while/body/eval_jaxpr/reduce_scatter | solution.py:267
  965.8 66.4 %reduce-scatter.26.cloned.1.call-start = ((), (), s32[]{:S(2)}) async-start(), calls=%async_computation.17 | async-start | bytes 884736
  968.3 129.9 %reduce-scatter.14.cloned.1.call-start = ((), (), s32[]{:S(2)}) async-start(), calls=%async_computation.11 | async-start | bytes 884736 | tf_op jit(solution)/shard_map/reduce_scatter | solution.py:316
  969.5 194.1 %reduce-scatter.16.cloned.1.call-start = ((), (), s32[]{:S(2)}) async-start(), calls=%async_computation.12 | async-start | bytes 884736 | tf_op jit(solution)/shard_map/reduce_scatter | solution.py:316
  970.8 258.7 %reduce-scatter.18.cloned.1.call-start = ((), (), s32[]{:S(2)}) async-start(), calls=%async_computation.13 | async-start | bytes 884736 | tf_op jit(solution)/shard_map/reduce_scatter | solution.py:316
  972.0 329.6 %reduce-scatter.20.cloned.1.call-start = ((), (), s32[]{:S(2)}) async-start(), calls=%async_computation.14 | async-start | bytes 2654208 | tf_op jit(solution)/shard_map/reduce_scatter | solution.py:316
  972.8 400.9 %reduce-scatter.22.cloned.1.call-start = ((), (), s32[]{:S(2)}) async-start(), calls=%async_computation.15 | async-start | bytes 2654208 | tf_op jit(solution)/shard_map/reduce_scatter | solution.py:316
  973.5 472.1 %reduce-scatter.24.cloned.1.call-start = ((), (), s32[]{:S(2)}) async-start(), calls=%async_computation.16 | async-start | bytes 2654208 | tf_op jit(solution)/shard_map/reduce_scatter | solution.py:319
  (152 other events, 2036.2 us)
Sparse Core Ops, SparseCore 0:
  17.2 21.3 all-gather.13
  134.7 27.7 reduce-scatter.27
  288.7 26.6 reduce-scatter.29
  352.2 28.1 reduce-scatter.31
  459.4 28.1 reduce-scatter.33
  491.9 19.6 all-gather.13
  608.6 27.4 reduce-scatter.27
  762.4 26.6 reduce-scatter.29
  825.9 28.1 reduce-scatter.31
  932.9 28.2 reduce-scatter.33
Sparse Core Ops, SparseCore 1:
  137.2 41.1 all-gather.17
  179.8 18.0 all-gather.15
  200.2 41.5 all-gather.19
  244.2 40.0 all-gather.21
  321.9 19.5 all-gather.23
  386.8 19.5 all-gather.25
  611.2 40.8 all-gather.17
  653.6 17.9 all-gather.15
  673.8 41.5 all-gather.19
  717.8 40.0 all-gather.21
  795.6 19.5 all-gather.23
  860.5 19.5 all-gather.25
  969.6 62.6 reduce-scatter.25
  1036.5 61.5 reduce-scatter.13
  1102.0 61.5 reduce-scatter.15
  1167.9 61.5 reduce-scatter.17
  1233.6 68.0 reduce-scatter.19
  1305.7 68.0 reduce-scatter.21
  1377.6 68.0 reduce-scatter.23
